TPU v7x, 512 devices: a whole 4x8x8 slice. The times are simulated.
512 devices in a mesh: ent: 128 (over y, z, core), rep: 4 (over x).
Axes of the slice: x: 4, y: 8, z: 8, core: 2. Of those that a mesh axis runs over, the one named last changes fastest.
Arguments:
- item_factors: bfloat16 [524288, 128], P(('ent', 'rep')), may hold values from -0.1 to 0.1
- tile_items: int32 [128, 4, 256, 32], P('ent', 'rep'), may hold values from 0 to 1023
- send_tiles: int32 [128, 4, 128], P('ent', 'rep'), may hold values from 1 to 2, as said below
- tile_users: int32 [128, 4, 256, 1], P('ent', 'rep'), may hold values from 0 to 7
- tile_counts: int32 [128, 4, 256, 32], P('ent', 'rep'), may hold values from 0 to 31
- recv_tiles: int32 [128, 4, 128], P('ent', 'rep'), may hold values from 1 to 2, as said below
Outputs:
- user_factors: float32 [1024, 128], P(('ent', 'rep'))
- item_rhs: float32 [524288, 128], P(('ent', 'rep'))
Inputs may be any that keep to these rules, and one draw needn't show every extreme that they name: send_tiles[e, r, p] counts the leading tile slots p * 2 to p * 2 + 1 of device (e, r) that are live; every device sends 2 tiles to some peer and receives 2 tiles from some peer. recv_tiles[p, r, e] equals send_tiles[e, r, p].
All inputs are finite; a program needn't handle non-finite values.
Results may differ from a plain program's by a relative error of at most 0.0009.
The roundings to bfloat16 on the way count: a program that leaves them out, or rounds other values in their place, can miss the bound.
Values may be sent and summed in bfloat16 or wider, within the bound.
A program may use at most 64 MiB of HBM per device.

v0:
```python
import jax
import jax.numpy as jnp
from jax import lax
from jax.sharding import PartitionSpec as P

U_DEV = 2
ALPHA = 40.0
RIDGE = 1.0
RHS_SCALE = 1.0 / 640.0


def solve_users(gram, rhs):
    lower = jnp.linalg.cholesky(gram)
    halfway = lax.linalg.triangular_solve(lower, rhs[..., None], left_side=True, lower=True)
    result = lax.linalg.triangular_solve(
        lower, halfway, left_side=True, lower=True, transpose_a=True
    )
    return result[..., 0]


def shards(item_factors, tile_items, send_tiles, tile_users, tile_counts, recv_tiles):
    highest = lax.Precision.HIGHEST
    rank_width = item_factors.shape[1]
    item_count = item_factors.shape[0]
    n_ent = lax.axis_size("ent")
    tile_slots = tile_items.shape[2]
    tile_rows = tile_items.shape[3]
    seg_count = tile_users.shape[3]
    seg_length = tile_rows // seg_count
    slot_cap = tile_slots // n_ent
    user_block = U_DEV * lax.axis_size("rep")
    item_ids = tile_items.reshape(tile_slots, tile_rows)
    slot_pos = jnp.arange(tile_slots, dtype=jnp.int32) % slot_cap
    live_send = slot_pos < jnp.repeat(send_tiles.reshape(n_ent), slot_cap)
    live_recv = slot_pos < jnp.repeat(recv_tiles.reshape(n_ent), slot_cap)
    partial_gram = lax.dot_general(
        item_factors, item_factors, (((0,), (0,)), ((), ())), preferred_element_type=jnp.float32
    )
    picked = jnp.take(item_factors, item_ids.reshape(-1), axis=0).reshape(
        tile_slots, tile_rows, rank_width
    )
    picked = jnp.where(live_send[:, None, None], picked, jnp.zeros((), jnp.bfloat16))
    incoming = lax.all_to_all(
        picked.reshape(n_ent, slot_cap * tile_rows, rank_width),
        "ent",
        split_axis=0,
        concat_axis=0,
        tiled=True,
    )
    counts_int = tile_counts.reshape(tile_slots, tile_rows)
    counts_f = counts_int.astype(jnp.float32)
    gram_weight = ALPHA * counts_f
    rhs_weight = jnp.where(
        live_recv[:, None] & (counts_int > 0), 1.0 + ALPHA * counts_f, jnp.float32(0.0)
    )
    owners = tile_users.reshape(tile_slots * seg_count)
    selector = owners[None, :] == jnp.arange(user_block, dtype=jnp.int32)[:, None]
    selector_f = selector.astype(jnp.float32)
    src_group = 1
    while (
        src_group * 2 <= n_ent
        and n_ent % (src_group * 2) == 0
        and (src_group * 2 * slot_cap * tile_rows <= 4096)
    ):
        src_group = src_group * 2
    tiles_blk = src_group * slot_cap
    block_count = tile_slots // tiles_blk
    runs_blk = tiles_blk * seg_count

    def accumulate(state_pair, pieces):
        gram_run, rhs_run = state_pair
        rows_blk, gram_blk, rhs_blk, select_blk = pieces
        weighted = (gram_blk[:, :, None] * rows_blk).astype(jnp.bfloat16)
        rows_seg = rows_blk.reshape(tiles_blk, seg_count, seg_length, rank_width)
        weighted = weighted.reshape(tiles_blk, seg_count, seg_length, rank_width)
        run_gram = jnp.einsum(
            "tsri,tsrj->tsij", weighted, rows_seg, preferred_element_type=jnp.float32
        )
        run_gram = run_gram.reshape(runs_blk, rank_width * rank_width)
        run_rhs = jnp.einsum(
            "tsr,tsri->tsi",
            rhs_blk.reshape(tiles_blk, seg_count, seg_length),
            rows_seg.astype(jnp.float32),
            precision=highest,
        )
        run_rhs = run_rhs.reshape(runs_blk, rank_width)
        gram_run = gram_run + jnp.dot(select_blk, run_gram, precision=highest)
        rhs_run = rhs_run + jnp.dot(select_blk, run_rhs, precision=highest)
        return ((gram_run, rhs_run), None)

    block_pieces = (
        incoming.reshape(block_count, tiles_blk, tile_rows, rank_width),
        gram_weight.reshape(block_count, tiles_blk, tile_rows),
        rhs_weight.reshape(block_count, tiles_blk, tile_rows),
        jnp.transpose(selector_f.reshape(user_block, block_count, runs_blk), (1, 0, 2)),
    )
    start_pair = (
        jnp.zeros((user_block, rank_width * rank_width), jnp.float32),
        jnp.zeros((user_block, rank_width), jnp.float32),
    )
    (gram_acc, rhs_acc), _ = lax.scan(accumulate, start_pair, block_pieces)
    identity_mat = jnp.eye(rank_width, dtype=jnp.float32)
    added_term = lax.psum(partial_gram, ("ent", "rep")) + RIDGE * identity_mat
    own_gram, own_rhs = (
        lax.psum_scatter(gram_acc, "rep", scatter_dimension=0, tiled=True),
        lax.psum_scatter(rhs_acc, "rep", scatter_dimension=0, tiled=True),
    )
    own_factors = solve_users(own_gram.reshape(-1, rank_width, rank_width) + added_term, own_rhs)
    solved = lax.all_gather(own_factors.astype(jnp.bfloat16), "rep", axis=0, tiled=True)
    run_factor = lax.dot_general(
        selector.astype(jnp.bfloat16),
        solved,
        (((0,), (0,)), ((), ())),
        preferred_element_type=jnp.float32,
    )
    back_factor, back_weight = (
        lax.all_to_all(
            run_factor.reshape(n_ent, slot_cap, seg_count * rank_width),
            "ent",
            split_axis=0,
            concat_axis=0,
            tiled=True,
        ),
        lax.all_to_all(
            rhs_weight.reshape(n_ent, slot_cap, tile_rows),
            "ent",
            split_axis=0,
            concat_axis=0,
            tiled=True,
        ),
    )

    def spread(running, pieces):
        factor_blk, weight_blk, item_blk = pieces
        contrib = (weight_blk[:, :, :, None] * factor_blk[:, :, None, :]).reshape(-1, rank_width)
        return (
            running + jax.ops.segment_sum(contrib, item_blk.reshape(-1), num_segments=item_count),
            None,
        )

    spread_pieces = (
        back_factor.reshape(block_count, tiles_blk, seg_count, rank_width),
        back_weight.reshape(block_count, tiles_blk, seg_count, seg_length),
        item_ids.reshape(block_count, tiles_blk, tile_rows),
    )
    item_rhs, _ = lax.scan(spread, jnp.zeros((item_count, rank_width), jnp.float32), spread_pieces)
    return (own_factors, item_rhs * RHS_SCALE)


def solution(mesh):
    in_specs = (
        P(("ent", "rep"), None),
        P("ent", "rep", None, None),
        P("ent", "rep", None),
        P("ent", "rep", None, None),
        P("ent", "rep", None, None),
        P("ent", "rep", None),
    )
    out_specs = (P(("ent", "rep"), None), P(("ent", "rep"), None))
    return jax.shard_map(shards, mesh=mesh, in_specs=in_specs, out_specs=out_specs, check_vma=False)
```

profile of v0, /device:TPU:1, one launch (start us, length us, event | category | flops | bytes accessed | tf_op | source)
XLA Modules:
  0.0 525.8 jit_solution(16828590585126697929)
XLA Ops:
  7.2 0.9 copy.43
  8.4 0.7 broadcast_compare_fusion.2
  9.2 24.0 %gather_fusion = bf16[8192,128]{1,0:T(8,128)(2,1)S(1)} fusion(bf16[1024,128]{1,0:T(8,128)(2,1)S(1)} %copy-done, s32[8192]{0:T(1024)S(1)} %broadcast_clamp_fusion), kind=kCustom, calls=%fused_computation | custom fusion | bytes 4227072 | tf_op jit(solution)/shard_map/jit(_take)/gather | solution.py:39
  33.2 4.6 select_select_fusion
  37.8 18.6 %all-to-all-start = ((bf16[128,64,128]{2,1,0:T(8,128)(2,1)}), bf16[128,64,128]{2,1,0:T(8,128)(2,1)S(1)}, u32[]{:S(2)}, u32[]{:S(2)}) async-start(bf16[128,64,128]{2,1,0:T(8,128)(2,1)} %select_select_fusion), calls=%async_computation | async-start | bytes 4194304 | tf_op jit(solution)/shard_map/all_to_all | solution.py:43
  56.4 0.9 fusion.25
  57.9 0.7 reduce.9
  59.4 1.3 dynamic-slice
  61.5 0.9 and_select_fusion
  62.4 46.3 %all-to-all-done = bf16[128,64,128]{2,1,0:T(8,128)(2,1)S(1)} async-done(((bf16[128,64,128]{2,1,0:T(8,128)(2,1)}), bf16[128,64,128]{2,1,0:T(8,128)(2,1)S(1)}, u32[]{:S(2)}, u32[]{:S(2)}) %all-to-all-start) | async-done | bytes 2097184 | tf_op jit(solution)/shard_map/all_to_all | solution.py:43
  108.7 7.6 %all-to-all-start.1 = ((f32[128,2,32]{2,1,0:T(2,128)}), f32[128,2,32]{2,1,0:T(2,128)S(1)}, u32[]{:S(2)}, u32[]{:S(2)}) async-start(f32[128,2,32]{2,1,0:T(2,128)} %and_select_fusion), calls=%async_computation.1 | async-start | bytes 262144 | tf_op jit(solution)/shard_map/all_to_all | solution.py:124
  116.5 37.8 %while.24 = (s32[]{:T(128)}, f32[8,16384]{1,0:T(8,128)S(1)}, f32[8,128]{1,0:T(8,128)S(1)}, f32[2,8,128]{2,1,0:T(8,128)S(1)}, f32[2,128,32]{2,1,0:T(8,128)S(1)}, ...) while((s32[]{:T(128)}, f32[8,16384]{1,0:T(8,128)S(1)}, ...), condition=%wide.region_1.2_spmd.clone, body=%wide.region_0.1_spmd.clone.sunk | while | flops 345245696 | bytes 21267580 | solution.py:101
  116.5 5.2 fusion.49
  121.7 12.5 %convolution_add_fusion.4 = f32[8,16384]{1,0:T(8,128)S(1)} fusion(f32[16,8,128,128]{3,2,1,0:T(8,128)} %bitcast.121, f32[8,16384]{1,0:T(8,128)S(1)} %get-tuple-element.219, pred[]{:T(512)S(6)} %compare.15, f32[2,8,128]{2,1,0:T(8,128)S(1)} %get-tuple-element.230, s32[]{:T(128)} %get-tuple-element.218), kind=kOutput, calls=%fused_computation.6.clone.1 | convolution fusion | flops 201588736 | bytes 9441285 | tf_op jit(solution)/shard_map/while/body/eval_jaxpr/dot_general | solution.py:87
  134.3 0.9 fusion.50
  135.4 5.2 fusion.49
  140.6 12.5 %convolution_add_fusion.4 = f32[8,16384]{1,0:T(8,128)S(1)} fusion(f32[16,8,128,128]{3,2,1,0:T(8,128)} %bitcast.121, f32[8,16384]{1,0:T(8,128)S(1)} %get-tuple-element.219, pred[]{:T(512)S(6)} %compare.15, f32[2,8,128]{2,1,0:T(8,128)S(1)} %get-tuple-element.230, s32[]{:T(128)} %get-tuple-element.218), kind=kOutput, calls=%fused_computation.6.clone.1 | convolution fusion | flops 201588736 | bytes 9441285 | tf_op jit(solution)/shard_map/while/body/eval_jaxpr/dot_general | solution.py:87
  153.2 0.9 fusion.50
  154.3 0.8 copy-done.1
  155.2 186.7 %all-reduce.5.cloned.1.call-done = f32[128,128]{1,0:T(8,128)} async-done(((f32[128,128]{1,0:T(8,128)}), f32[128,128]{1,0:T(8,128)}) %all-reduce.5.cloned.1.call-update) | async-done | bytes 65552 | tf_op jit(solution)/shard_map/psum | solution.py:103
  341.9 0.9 convert_add_fusion
  342.9 8.1 %all-reduce.1 = f32[8,128]{1,0:T(8,128)S(1)} all-reduce(f32[8,128]{1,0:T(8,128)S(1)} %get-tuple-element.68), channel_id=3, replica_groups=mesh['ent'=128,'rep'=4] {'rep'}, use_global_device_ids=true, to_apply=%region_6.7.clone | all-reduce | flops 1024 | bytes 8192
  350.9 37.3 %all-reduce.7.cloned.1.call-done = f32[8,16384]{1,0:T(8,128)} async-done(((f32[8,16384]{1,0:T(8,128)}), f32[8,16384]{1,0:T(8,128)}) %all-reduce.7.cloned.1.call-update) | async-done | bytes 524304
  388.3 1.1 dynamic-slice_bitcast_fusion.2
  389.6 23.5 %custom-call.9 = f32[2,128,128]{2,1,0:T(8,128)S(1)} custom-call(f32[2,128,128]{2,1,0:T(8,128)S(1)} %fusion.20), custom_call_target="Cholesky" | custom-call | tf_op jit(solution)/shard_map/jit(cholesky)/cholesky | solution.py:13
  413.3 19.7 %custom-call.10 = f32[2,1,128,128]{2,3,1,0:T(8,128)S(1)} custom-call(f32[2,1,128,128]{3,2,1,0:T(8,128)S(1)} %select_bitcast_fusion), custom_call_target="InvertDiagBlocksLowerTriangular" | custom-call | tf_op jit(solution)/shard_map/triangular_solve | solution.py:15
  433.6 6.8 %all-gather = bf16[4,2,128]{2,1,0:T(2,128)(2,1)S(1)} all-gather(bf16[1,2,128]{2,1,0:T(2,128)(2,1)S(1)} %convert_bitcast_fusion), channel_id=1, replica_groups=mesh['ent'=128,'rep'=4] {'rep'}, dimensions={0}, use_global_device_ids=true | all-gather | bytes 2560 | tf_op jit(solution)/shard_map/all_gather | solution.py:109
  440.6 30.5 %all_to_all.15 = f32[128,2,128]{2,1,0:T(2,128)S(1)} all-to-all(f32[128,2,128]{2,1,0:T(2,128)S(1)} %bitcast.132), channel_id=1, replica_groups=mesh['ent'=128,'rep'=4] {'ent'}, dimensions={0} | all-to-all | bytes 262144 | tf_op jit(solution)/shard_map/all_to_all | solution.py:117
  471.2 46.8 %while.23 = (s32[]{:T(128)}, f32[1024,128]{1,0:T(8,128)S(1)}, s32[2,128,32]{2,1,0:T(8,128)S(1)}, f32[2,128,1,32]{3,1,2,0:T(8,128)S(1)}, f32[2,128,1,128]{3,1,2,0:T(8,128)S(1)}, /*index=5*/s32[]{:T(128)}) while((s32[]{:T(128)}, f32[1024,128]{1,0:T(8,128)S(1)}, s32[2,128,32]{2,1,0:T(8,128)S(1)}, f32[2,128,1,32]{3,1,2,0:T(8,128)S(1)}, ...), condition=%wide.region_9.10_spmd, body=%wide.region_7.9_spmd.sunk | while | flops 1048578 | bytes 8749137 | solution.py:146
  472.1 22.6 %scatter_fusion = f32[1024,128]{1,0:T(8,128)S(1)} fusion(f32[1024,128]{1,0:T(8,128)S(1)} %get-tuple-element.243, s32[4096]{0:T(1024)S(1)} %reshape.259, f32[4096,128]{1,0:T(8,128)S(1)} %bitcast_multiply_fusion.2), kind=kCustom, calls=%fused_computation.1.clone.1 | custom fusion | flops 524288 | bytes 6307840 | tf_op jit(solution)/shard_map/while/body/eval_jaxpr/scatter-add | solution.py:137
  495.5 22.6 %scatter_fusion = f32[1024,128]{1,0:T(8,128)S(1)} fusion(f32[1024,128]{1,0:T(8,128)S(1)} %get-tuple-element.243, s32[4096]{0:T(1024)S(1)} %reshape.259, f32[4096,128]{1,0:T(8,128)S(1)} %bitcast_multiply_fusion.2), kind=kCustom, calls=%fused_computation.1.clone.1 | custom fusion | flops 524288 | bytes 6307840 | tf_op jit(solution)/shard_map/while/body/eval_jaxpr/scatter-add | solution.py:137
  518.1 0.8 broadcast_multiply_fusion
  (75 shorter events, 5.6 us)
Async XLA Ops:
  7.2 2.0 copy-start
  37.8 20.1 %copy-start.5 = (s32[1,1,128]{2,1,0:T(1,128)S(1)}, s32[1,1,128]{2,1,0:T(1,128)}, u32[]{:S(2)}) copy-start(s32[1,1,128]{2,1,0:T(1,128)} %param.15) | copy-start | bytes 1540
  37.8 21.0 %copy-start.2 = (s32[1,1,256,32]{2,3,1,0:T(8,128)S(1)}, s32[1,1,256,32]{2,3,1,0:T(8,128)}, u32[]{:S(2)}) copy-start(s32[1,1,256,32]{2,3,1,0:T(8,128)} %param.14) | copy-start | bytes 98308
  37.8 23.6 %copy-start.3 = (s32[1,1,256,1]{2,3,1,0:T(1,128)S(1)}, s32[1,1,256,1]{2,3,1,0:T(1,128)}, u32[]{:S(2)}) copy-start(s32[1,1,256,1]{2,3,1,0:T(1,128)} %param.13) | copy-start | bytes 3076
  37.8 70.9 %all-to-all-start = ((bf16[128,64,128]{2,1,0:T(8,128)(2,1)}), bf16[128,64,128]{2,1,0:T(8,128)(2,1)S(1)}, u32[]{:S(2)}, u32[]{:S(2)}) async-start(bf16[128,64,128]{2,1,0:T(8,128)(2,1)} %select_select_fusion), calls=%async_computation | async-start | bytes 4194304 | tf_op jit(solution)/shard_map/all_to_all | solution.py:43
  56.4 285.5 %all-reduce.5.cloned.1.call-start = ((), (), s32[]{:S(2)}) async-start(), calls=%async_computation.3 | async-start | bytes 131072 | tf_op jit(solution)/shard_map/psum | solution.py:103
  108.7 332.0 %all-to-all-start.1 = ((f32[128,2,32]{2,1,0:T(2,128)}), f32[128,2,32]{2,1,0:T(2,128)S(1)}, u32[]{:S(2)}, u32[]{:S(2)}) async-start(f32[128,2,32]{2,1,0:T(2,128)} %and_select_fusion), calls=%async_computation.1 | async-start | bytes 262144 | tf_op jit(solution)/shard_map/all_to_all | solution.py:124
  116.3 272.0 %all-reduce.7.cloned.1.call-start = ((), (), s32[]{:S(2)}) async-start(), calls=%async_computation.4 | async-start | bytes 1048576
  154.3 0.8 copy-start.1
  433.6 37.7 %copy-start.4 = (f32[2,1,128]{2,1,0:T(1,128)}, f32[2,1,128]{2,1,0:T(1,128)S(1)}, u32[]{:S(2)}) copy-start(f32[2,1,128]{2,1,0:T(1,128)S(1)} %fusion.17) | copy-start | bytes 3076
Sparse Core Ops, SparseCore 0:
  62.2 279.6 all-reduce.4
  344.9 43.2 all-reduce.6
where the time goes:
time: 526 us
  waiting for transfers between devices  270 us (51%)
  other arithmetic  98.5 us (19%)
  blocking collectives  45.4 us (9%)
  matrix products  39.3 us (7%)
  local copies, waits for them, and re-layouts  30.6 us (6%)
  starting transfers between devices  26.4 us (5%)
  between operations  15 us (3%)
    psum x1, waiting for transfers between devices, shards(): added_term = lax.psum(partial_gram, ('ent', 'rep')) + RIDGE * identity_mat  187 us
    all_to_all x1, waiting for transfers between devices, shards(): lax.all_to_all(picked.reshape(n_ent, slot_cap * tile_rows, rank_width), '...  46.3 us
    scatter-add x2, other arithmetic, spread(): jax.ops.segment_sum(contrib, item_blk.reshape(-1), num_segments=item_count)  45.1 us
    unnamed x3, waiting for transfers between devices  37.4 us
    all_to_all x1, blocking collectives, shards(): lax.all_to_all(run_factor.reshape(n_ent, slot_cap, seg_count * rank_width...  30.5 us
    dot_general x2, matrix products, accumulate(): gram_run = gram_run + jnp.dot(select_blk, run_gram, precision=highest)  25 us
    gather x1, local copies, waits for them, and re-layouts, shards(): jnp.take(item_factors, item_ids.reshape(-1), axis=0)  24 us
    another operation x4, other arithmetic, solve_users(): lower = jnp.linalg.cholesky(gram)  23.6 us
  transfers between devices with their start and end apart: 4, of which 3 were waited for; matrix products, arithmetic and copies ran while one was open for 17% of the time, Pallas kernels for 0%

commit v1 on v0

--- a/solution.py
+++ b/solution.py
@@ -100,7 +100,9 @@
     )
     (gram_acc, rhs_acc), _ = lax.scan(accumulate, start_pair, block_pieces)
     identity_mat = jnp.eye(rank_width, dtype=jnp.float32)
-    added_term = lax.psum(partial_gram, ("ent", "rep")) + RIDGE * identity_mat
+    added_term = (
+        jnp.sum(lax.all_gather(partial_gram, ("ent", "rep")), axis=0) + RIDGE * identity_mat
+    )
     own_gram, own_rhs = (
         lax.psum_scatter(gram_acc, "rep", scatter_dimension=0, tiled=True),
         lax.psum_scatter(rhs_acc, "rep", scatter_dimension=0, tiled=True),

time: 526 us -> 441 us (0.84)
  waiting for transfers between devices: 270 us -> 189 us
  other arithmetic: 98.5 us -> 111 us
  matrix products: 39.3 us -> 27 us
  blocking collectives: 45.4 us -> 39.7 us
    psum x1 -> x0, waiting for transfers between devices: 187 us -> none  [shards(): added_term = lax.psum(partial_gram, ('ent', 'rep')) + RIDGE * identity_mat]
    all_gather x0 -> x1, waiting for transfers between devices: none -> 113 us  [shards(): lax.all_gather(partial_gram, ('ent', 'rep'))]
    reduce_sum x0 -> x1, other arithmetic: none -> 13.1 us  [shards(): jnp.sum(lax.all_gather(partial_gram, ('ent', 'rep')), axis=0)]
    unnamed x3, waiting for transfers between devices: 37.4 us -> 26.2 us
    dot_general x2, matrix products: 25 us -> 17.2 us  [accumulate(): gram_run = gram_run + jnp.dot(select_blk, run_gram, precision=highest)]
    all_to_all x1, blocking collectives: 30.5 us -> 24.9 us  [shards(): lax.all_to_all(run_factor.reshape(n_ent, slot_cap, seg_count * rank_width...]
  transfers between devices with their start and end apart: 4 -> 4, of which waited for: 3 -> 3; matrix products, arithmetic and copies ran while one was open for 17% -> 14% of each run, Pallas kernels for 0% -> 0%
where the time goes in v1:
time: 441 us
  waiting for transfers between devices  189 us (43%)
  other arithmetic  111 us (25%)
  blocking collectives  39.7 us (9%)
  local copies, waits for them, and re-layouts  30.5 us (7%)
  matrix products  27 us (6%)
  starting transfers between devices  26.4 us (6%)
  between operations  16.4 us (4%)
    all_gather x1, waiting for transfers between devices, shards(): lax.all_gather(partial_gram, ('ent', 'rep'))  113 us
    all_to_all x1, waiting for transfers between devices, shards(): lax.all_to_all(picked.reshape(n_ent, slot_cap * tile_rows, rank_width), '...  50.2 us
    scatter-add x2, other arithmetic, spread(): jax.ops.segment_sum(contrib, item_blk.reshape(-1), num_segments=item_count)  45.1 us
    unnamed x3, waiting for transfers between devices  26.2 us
    all_to_all x1, blocking collectives, shards(): lax.all_to_all(run_factor.reshape(n_ent, slot_cap, seg_count * rank_width...  24.9 us
    gather x1, local copies, waits for them, and re-layouts, shards(): jnp.take(item_factors, item_ids.reshape(-1), axis=0)  24 us
    another operation x4, other arithmetic, solve_users(): lower = jnp.linalg.cholesky(gram)  23.6 us
    another operation x3, other arithmetic, solve_users(): lax.linalg.triangular_solve(lower, halfway, left_side=True, lower=True, t...  19.8 us
  transfers between devices with their start and end apart: 4, of which 3 were waited for; matrix products, arithmetic and copies ran while one was open for 14% of the time, Pallas kernels for 0%

profile of v1, /device:TPU:1, one launch (start us, length us, event | category | flops | bytes accessed | tf_op | source)
XLA Modules:
  0.0 440.6 jit_solution(17424386163869746797)
XLA Ops:
  8.0 0.9 copy.43
  9.1 0.7 broadcast_compare_fusion.2
  10.0 24.0 %gather_fusion = bf16[8192,128]{1,0:T(8,128)(2,1)S(1)} fusion(bf16[1024,128]{1,0:T(8,128)(2,1)S(1)} %copy-done, s32[8192]{0:T(1024)S(1)} %broadcast_clamp_fusion), kind=kCustom, calls=%fused_computation | custom fusion | bytes 4227072 | tf_op jit(solution)/shard_map/jit(_take)/gather | solution.py:39
  34.1 4.6 %select_select_fusion = bf16[128,64,128]{2,1,0:T(8,128)(2,1)} fusion(bf16[128,64,128]{2,1,0:T(8,128)(2,1)S(1)} %bitcast.125, pred[128,64]{1,0:T(8,128)(4,1)S(1)} %compare_and_fusion, pred[128,64]{1,0:T(8,128)(4,1)S(1)} %copy.42), kind=kLoop, calls=%fused_computation.28 | loop fusion | flops 2097152 | bytes 4210688 | tf_op jit(solution)/shard_map/jit(_where)/select_n | solution.py:42
  38.6 18.6 %all-to-all-start = ((bf16[128,64,128]{2,1,0:T(8,128)(2,1)}), bf16[128,64,128]{2,1,0:T(8,128)(2,1)S(1)}, u32[]{:S(2)}, u32[]{:S(2)}) async-start(bf16[128,64,128]{2,1,0:T(8,128)(2,1)} %select_select_fusion), calls=%async_computation | async-start | bytes 4194304 | tf_op jit(solution)/shard_map/all_to_all | solution.py:43
  57.8 0.7 reduce.9
  59.1 50.2 %all-to-all-done = bf16[128,64,128]{2,1,0:T(8,128)(2,1)S(1)} async-done(((bf16[128,64,128]{2,1,0:T(8,128)(2,1)}), bf16[128,64,128]{2,1,0:T(8,128)(2,1)S(1)}, u32[]{:S(2)}, u32[]{:S(2)}) %all-to-all-start) | async-done | bytes 2097184 | tf_op jit(solution)/shard_map/all_to_all | solution.py:43
  109.3 25.7 %while.24 = (s32[]{:T(128)}, f32[8,16384]{1,0:T(8,128)S(1)}, f32[8,128]{1,0:T(8,128)S(1)}, f32[2,8,128]{2,1,0:T(8,128)S(1)}, f32[2,128,32]{2,1,0:T(8,128)S(1)}, ...) while((s32[]{:T(128)}, f32[8,16384]{1,0:T(8,128)S(1)}, ...), condition=%wide.region_1.2_spmd.clone, body=%wide.region_0.1_spmd.clone.sunk | while | flops 345245696 | bytes 21267588 | solution.py:101
  109.3 1.0 fusion.50
  110.5 2.9 fusion.49
  113.4 8.6 %convolution_add_fusion.4 = f32[8,16384]{1,0:T(8,128)S(1)} fusion(f32[16,8,128,128]{3,2,1,0:T(8,128)S(1)} %bitcast.122, f32[8,16384]{1,0:T(8,128)S(1)} %get-tuple-element.219, pred[]{:T(512)S(6)} %compare.15, f32[2,8,128]{2,1,0:T(8,128)S(1)} %get-tuple-element.230, s32[]{:T(128)S(6)} %copy.74), kind=kOutput, calls=%fused_computation.6.clone.1 | convolution fusion | flops 201588736 | bytes 9441285 | tf_op jit(solution)/shard_map/while/body/eval_jaxpr/dot_general | solution.py:87
  122.1 1.0 fusion.50
  123.2 2.9 fusion.49
  126.2 8.6 %convolution_add_fusion.4 = f32[8,16384]{1,0:T(8,128)S(1)} fusion(f32[16,8,128,128]{3,2,1,0:T(8,128)S(1)} %bitcast.122, f32[8,16384]{1,0:T(8,128)S(1)} %get-tuple-element.219, pred[]{:T(512)S(6)} %compare.15, f32[2,8,128]{2,1,0:T(8,128)S(1)} %get-tuple-element.230, s32[]{:T(128)S(6)} %copy.74), kind=kOutput, calls=%fused_computation.6.clone.1 | convolution fusion | flops 201588736 | bytes 9441285 | tf_op jit(solution)/shard_map/while/body/eval_jaxpr/dot_general | solution.py:87
  135.0 0.8 copy-done.1
  135.9 0.9 fusion.25
  137.1 0.8 and_select_fusion
  137.9 7.8 %all-to-all-start.1 = ((f32[128,2,32]{2,1,0:T(2,128)}), f32[128,2,32]{2,1,0:T(2,128)S(1)}, u32[]{:S(2)}, u32[]{:S(2)}) async-start(f32[128,2,32]{2,1,0:T(2,128)} %and_select_fusion), calls=%async_computation.1 | async-start | bytes 262144 | tf_op jit(solution)/shard_map/all_to_all | solution.py:126
  145.7 1.3 dynamic-slice
  147.7 9.1 %all-reduce.1 = f32[8,128]{1,0:T(8,128)S(1)} all-reduce(f32[8,128]{1,0:T(8,128)S(1)} %get-tuple-element.68), channel_id=4, replica_groups=mesh['ent'=128,'rep'=4] {'rep'}, use_global_device_ids=true, to_apply=%region_6.7.clone | all-reduce | flops 1024 | bytes 8192
  156.8 26.2 %all-reduce.4.cloned.1.call-done = f32[8,16384]{1,0:T(8,128)} async-done(((f32[8,16384]{1,0:T(8,128)}), f32[8,16384]{1,0:T(8,128)}) %all-reduce.4.cloned.1.call-update) | async-done | bytes 524304
  183.0 1.1 dynamic-slice_bitcast_fusion.2
  184.2 113.0 %all-gather.4.cloned.1.call-done = f32[65536,128]{1,0:T(8,128)} async-done(((f32[128,128]{1,0:T(8,128)}), f32[65536,128]{1,0:T(8,128)}) %all-gather.4.cloned.1.call-update) | async-done | bytes 33554448 | tf_op jit(solution)/shard_map/all_gather | solution.py:104
  297.2 13.1 %reduce_sum.9 = f32[128,128]{1,0:T(8,128)S(1)} reduce(f32[512,128,128]{2,1,0:T(8,128)} %bitcast.124, f32[]{:T(128)} %constant.109.clone.1), dimensions={0}, to_apply=%region_3.4 | reduce | flops 8372224 | bytes 33619972 | tf_op jit(solution)/shard_map/reduce_sum | solution.py:104
  310.6 23.5 %custom-call.9 = f32[2,128,128]{2,1,0:T(8,128)S(1)} custom-call(f32[2,128,128]{2,1,0:T(8,128)S(1)} %fusion.20), custom_call_target="Cholesky" | custom-call | tf_op jit(solution)/shard_map/jit(cholesky)/cholesky | solution.py:13
  334.3 19.7 %custom-call.10 = f32[2,1,128,128]{2,3,1,0:T(8,128)S(1)} custom-call(f32[2,1,128,128]{3,2,1,0:T(8,128)S(1)} %select_bitcast_fusion), custom_call_target="InvertDiagBlocksLowerTriangular" | custom-call | tf_op jit(solution)/shard_map/triangular_solve | solution.py:15
  354.5 5.7 %all-gather.1 = bf16[4,2,128]{2,1,0:T(2,128)(2,1)S(1)} all-gather(bf16[1,2,128]{2,1,0:T(2,128)(2,1)S(1)} %convert_bitcast_fusion), channel_id=1, replica_groups=mesh['ent'=128,'rep'=4] {'rep'}, dimensions={0}, use_global_device_ids=true | all-gather | bytes 2560 | tf_op jit(solution)/shard_map/all_gather | solution.py:111
  360.5 24.9 %all_to_all.15 = f32[128,2,128]{2,1,0:T(2,128)S(1)} all-to-all(f32[128,2,128]{2,1,0:T(2,128)S(1)} %bitcast.134), channel_id=1, replica_groups=mesh['ent'=128,'rep'=4] {'ent'}, dimensions={0} | all-to-all | bytes 262144 | tf_op jit(solution)/shard_map/all_to_all | solution.py:119
  385.4 46.8 %while.23 = (s32[]{:T(128)}, f32[1024,128]{1,0:T(8,128)S(1)}, s32[2,128,32]{2,1,0:T(8,128)S(1)}, f32[2,128,1,32]{3,1,2,0:T(8,128)S(1)}, f32[2,128,1,128]{3,1,2,0:T(8,128)S(1)}, /*index=5*/s32[]{:T(128)}) while((s32[]{:T(128)}, f32[1024,128]{1,0:T(8,128)S(1)}, s32[2,128,32]{2,1,0:T(8,128)S(1)}, f32[2,128,1,32]{3,1,2,0:T(8,128)S(1)}, ...), condition=%wide.region_9.10_spmd, body=%wide.region_7.9_spmd.sunk | while | flops 1048578 | bytes 8749145 | solution.py:148
  386.3 22.6 %scatter_fusion = f32[1024,128]{1,0:T(8,128)S(1)} fusion(f32[1024,128]{1,0:T(8,128)S(1)} %get-tuple-element.243, s32[4096]{0:T(1024)S(1)} %reshape.270, f32[4096,128]{1,0:T(8,128)S(1)} %bitcast_multiply_fusion.2), kind=kCustom, calls=%fused_computation.1.clone.1 | custom fusion | flops 524288 | bytes 6307840 | tf_op jit(solution)/shard_map/while/body/eval_jaxpr/scatter-add | solution.py:139
  409.7 22.6 %scatter_fusion = f32[1024,128]{1,0:T(8,128)S(1)} fusion(f32[1024,128]{1,0:T(8,128)S(1)} %get-tuple-element.243, s32[4096]{0:T(1024)S(1)} %reshape.270, f32[4096,128]{1,0:T(8,128)S(1)} %bitcast_multiply_fusion.2), kind=kCustom, calls=%fused_computation.1.clone.1 | custom fusion | flops 524288 | bytes 6307840 | tf_op jit(solution)/shard_map/while/body/eval_jaxpr/scatter-add | solution.py:139
  432.3 0.8 broadcast_multiply_fusion
  (76 shorter events, 5.4 us)
Async XLA Ops:
  8.0 2.0 copy-start
  38.6 19.1 %copy-start.5 = (s32[1,1,128]{2,1,0:T(1,128)S(1)}, s32[1,1,128]{2,1,0:T(1,128)}, u32[]{:S(2)}) copy-start(s32[1,1,128]{2,1,0:T(1,128)} %param.15) | copy-start | bytes 1540
  38.6 19.9 %copy-start.2 = (s32[1,1,256,32]{2,3,1,0:T(8,128)S(1)}, s32[1,1,256,32]{2,3,1,0:T(8,128)}, u32[]{:S(2)}) copy-start(s32[1,1,256,32]{2,3,1,0:T(8,128)} %param.14) | copy-start | bytes 98308
  38.6 20.4 %copy-start.3 = (s32[1,1,256,1]{2,3,1,0:T(1,128)S(1)}, s32[1,1,256,1]{2,3,1,0:T(1,128)}, u32[]{:S(2)}) copy-start(s32[1,1,256,1]{2,3,1,0:T(1,128)} %param.13) | copy-start | bytes 3076
  38.6 70.7 %all-to-all-start = ((bf16[128,64,128]{2,1,0:T(8,128)(2,1)}), bf16[128,64,128]{2,1,0:T(8,128)(2,1)S(1)}, u32[]{:S(2)}, u32[]{:S(2)}) async-start(bf16[128,64,128]{2,1,0:T(8,128)(2,1)} %select_select_fusion), calls=%async_computation | async-start | bytes 4194304 | tf_op jit(solution)/shard_map/all_to_all | solution.py:43
  57.2 125.8 %all-reduce.4.cloned.1.call-start = ((), (), s32[]{:S(2)}) async-start(), calls=%async_computation.4 | async-start | bytes 1048576
  135.0 0.8 copy-start.1
  135.8 161.4 %all-gather.4.cloned.1.call-start = ((), (), s32[]{:S(2)}) async-start(), calls=%async_computation.3 | async-start | bytes 33619968 | tf_op jit(solution)/shard_map/all_gather | solution.py:104
  137.9 222.6 %all-to-all-start.1 = ((f32[128,2,32]{2,1,0:T(2,128)}), f32[128,2,32]{2,1,0:T(2,128)S(1)}, u32[]{:S(2)}, u32[]{:S(2)}) async-start(f32[128,2,32]{2,1,0:T(2,128)} %and_select_fusion), calls=%async_computation.1 | async-start | bytes 262144 | tf_op jit(solution)/shard_map/all_to_all | solution.py:126
  354.5 30.9 %copy-start.4 = (f32[2,1,128]{2,1,0:T(1,128)}, f32[2,1,128]{2,1,0:T(1,128)S(1)}, u32[]{:S(2)}) copy-start(f32[2,1,128]{2,1,0:T(1,128)S(1)} %fusion.17) | copy-start | bytes 3076
Sparse Core Ops, SparseCore 0:
  135.9 46.9 all-reduce.3
Sparse Core Ops, SparseCore 1:
  140.7 156.4 all-gather.3
